TPU v7x, 32 devices: a whole 2x2x4 slice. The times are simulated.
32 devices in a mesh: section: 2 (over core), dp: 4 (over y, x), tensor: 4 (over z).
Axes of the slice: x: 2, y: 2, z: 4, core: 2. Of those that a mesh axis runs over, the one named last changes fastest.
Arguments:
- section_input: bfloat16 [2, 512, 4096], P('section', 'dp'), may hold values from -60 to 60
- weights: bfloat16 [2, 4096, 4096], P('section', 'tensor', 'dp'), may hold values from -0.1875 to 0.1875
- gains: float32 [2, 4096], P('section'), may hold values from 0.1 to 1.9
- proj_seeds: int32 [2, 2], P('section'), may hold values from 0 to 99999
- out_grad: bfloat16 [512, 4096], P('dp'), may hold values from -0.75 to 0.75
- query_grads: bfloat16 [2, 256, 4096], P('section', 'dp', 'tensor'), may hold values from -0.017944336 to 0.017944336
Outputs:
- projected_grads: float32 [2, 2, 4096], P('section', None, 'tensor')
- scores: float32 [2, 256], P(None, 'dp')
All inputs are finite; a program needn't handle non-finite values.
Results may differ from a plain program's by a relative error of at most 0.033.
Values may be sent and summed in bfloat16 or wider, within the bound.
A program may use at most 64 MiB of HBM per device.

v0:
```python
import functools
import math

import jax
import jax.numpy as jnp
from jax import lax
from jax.experimental import pallas as pl
from jax.experimental.pallas import tpu as pltpu
from jax.sharding import PartitionSpec as P

R = 64
SEQS = 2
eps = 1e-05
F32 = jnp.float32
BF16 = jnp.bfloat16
MESH = pl.DeviceIdType.MESH
NT = (((1,), (1,)), ((), ()))


def sign_rows(seed_value, row_start, row_count, scale):
    row_index = lax.broadcasted_iota(jnp.int32, (R, row_count), 1) + row_start
    col_index = lax.broadcasted_iota(jnp.int32, (R, row_count), 0)
    mixing = row_index * 40503 + col_index * 9973 + (seed_value * 7919 + 12345)
    mixing = mixing ^ (mixing >> 13)
    mixing = mixing * 1274126177
    mixing = mixing ^ (mixing >> 16)
    parity = (mixing >> 10) & 1
    return jnp.where(parity == 1, scale, -scale).astype(BF16)


def kernel(
    sections, nd, nz,
    x_hbm, w_hbm, gain_ref, seed_ref, og_ref, q_ref,
    out_ref,
    a_buf, inf_buf, ps_buf, pr_buf, slope_buf, ui_buf, uii_buf, gp_buf,
    gns_buf, gnr_buf, dot_buf, up_buf, g_buf, gr_buf, sc_buf,
    x_ref, w_ref, sum_buf, norm_buf, rad_buf, turn_buf, mean_buf, left_buf, pick_buf,
    a_ss, a_rs, inf_ss, inf_rs, p_ss, p_rs, og_ss, og_rs, gp_ss, gp_rs,
    gn_ss, gn_rs, dt_ss, dt_rs, up_ss, up_rs, uii_ss, uii_rs,
    g_ss, g_rs, sc_ss, sc_rs, in_sem, go_sem, far_sem,
):
    s = lax.axis_index("section")
    d = lax.axis_index("dp")
    z = lax.axis_index("tensor")
    tok, width = x_hbm.shape
    feat = width // nz
    cols = width // nd
    sub = tok // nz
    at_top = s == sections - 1
    below_top = s == sections - 2
    lower = s > 0
    z_start = pl.multiple_of(z * feat, feat)
    d_start = pl.multiple_of(d * cols, cols)
    sub_start = pl.multiple_of(z * sub, sub)
    sub_start_d = pl.multiple_of(d * sub, sub)

    def dev(s_to, d_to, z_to):
        return {"section": s_to, "dp": d_to, "tensor": z_to}

    def remote(src, dst, ss, rs, to):
        return pltpu.make_async_remote_copy(
            src_ref=src, dst_ref=dst, send_sem=ss, recv_sem=rs, device_id=to, device_id_type=MESH
        )

    x_load = pltpu.make_async_copy(x_hbm, x_ref, in_sem.at[0])
    w_load = pltpu.make_async_copy(w_hbm, w_ref, in_sem.at[1])
    x_load.start()
    w_load.start()

    barrier = pltpu.get_barrier_semaphore()
    column = sections * nz
    here = s * nz + z

    def signal_column(sem):
        for o in range(1, column):
            to = lax.rem(here + o, column)
            pl.semaphore_signal(
                sem, inc=1, device_id=dev(to // nz, d, lax.rem(to, nz)), device_id_type=MESH
            )

    for o in range(1, nd):
        pl.semaphore_signal(
            barrier, inc=1, device_id=dev(s, lax.rem(d + o, nd), z), device_id_type=MESH
        )
    signal_column(barrier)

    x_load.wait()
    hidden = x_ref[...].astype(F32)
    radius = jnp.sqrt(jnp.mean(hidden * hidden, axis=1, keepdims=True) + eps)
    gain_z = gain_ref[:, pl.ds(z_start, feat)]
    normed_z = x_ref[:, pl.ds(z_start, feat)].astype(F32) / radius
    norm_buf[...] = normed_z
    rad_buf[...] = jnp.broadcast_to(radius, rad_buf.shape)
    a_buf[d] = (normed_z * gain_z).astype(BF16)

    pl.semaphore_wait(barrier, nd - 1 + column - 1)

    def a_copy(o):
        to = lax.rem(d + o, nd)
        return remote(a_buf.at[d], a_buf.at[d], a_ss.at[o], a_rs.at[o], dev(s, to, z))

    @pl.when(jnp.logical_not(below_top))
    def _():
        for o in range(1, nd):
            a_copy(o).start()

    def og_copy(o):
        to = lax.rem(d + o, nd)
        src = og_ref.at[pl.ds(sub_start, sub), pl.ds(pl.multiple_of(to * cols, cols), cols)]
        return remote(src, ui_buf.at[d], og_ss.at[o], og_rs.at[o], dev(s, to, z))

    def ui_load():
        src = og_ref.at[pl.ds(sub_start, sub), pl.ds(d_start, cols)]
        return pltpu.make_async_copy(src, ui_buf.at[d], in_sem.at[2])

    def uii_load():
        return pltpu.make_async_copy(og_ref.at[:, pl.ds(z_start, feat)], uii_buf, in_sem.at[3])

    @pl.when(at_top)
    def _():
        for o in range(1, nd):
            og_copy(o).start()
        ui_load().start()
        uii_load().start()

    @pl.when(below_top)
    def _():
        pl.semaphore_wait(go_sem.at[0], 1)
        for o in range(1, nd):
            a_copy(o).start()

    signal_column(far_sem.at[0])

    w_load.wait()

    def p_copy(o, block):
        to = lax.rem(z + o, nz)
        return remote(
            ps_buf.at[to, block], pr_buf.at[z, block], p_ss.at[o, block], p_rs.at[o, block],
            dev(s, d, to),
        )

    for o in range(nd):
        block = lax.rem(d + nd - o, nd)
        if o:
            a_copy(o).wait_recv()
        part = jnp.dot(a_buf[block], w_ref[...], preferred_element_type=F32).astype(BF16)
        for zt in range(nz):
            ps_buf[zt, block] = part[zt * sub : (zt + 1) * sub, :]

        @pl.when(jnp.logical_not(below_top))
        def _():
            for oz in range(1, nz):
                p_copy(oz, block).start()

    for o in range(1, nd):
        a_copy(o).wait_send()

    def go(which):
        pl.semaphore_signal(
            go_sem.at[which], inc=1, device_id=dev(jnp.maximum(s - 1, 0), d, z), device_id_type=MESH
        )

    if sections > 1:
        @pl.when(at_top)
        def _():
            go(0)

    scale = 1.0 / math.sqrt(width)
    x_sub = x_ref[pl.ds(sub_start, sub), :].astype(F32)
    radius_sub = jnp.sqrt(jnp.mean(x_sub * x_sub, axis=1, keepdims=True) + eps)
    lifted_sub = (x_sub / radius_sub * gain_ref[...]).astype(BF16)
    table_in = sign_rows(seed_ref[0, 0], 0, width, scale)
    inf_buf[d] = lax.dot_general(lifted_sub, table_in, NT, preferred_element_type=F32)

    def inf_copy(o):
        to = lax.rem(d + o, nd)
        return remote(inf_buf.at[d], inf_buf.at[d], inf_ss.at[o], inf_rs.at[o], dev(s, to, z))

    for o in range(1, nd):
        inf_copy(o).start()


    piece = R * R // nz
    per_seq = nd * sub // SEQS

    def spread():
        for o in range(1, nd):
            inf_copy(o).wait_recv()
        in_feat = inf_buf[...].reshape(nd * sub, R).astype(BF16)
        for zt in range(nz):
            entry = lax.broadcasted_iota(jnp.int32, (R, piece), 1) + zt * piece
            which = lax.broadcasted_iota(jnp.int32, (R, piece), 0)
            pick_in = (entry // R == which).astype(F32).astype(BF16)
            pick_buf[zt] = (entry % R == which).astype(F32).astype(BF16)
            left_buf[zt] = jnp.dot(in_feat, pick_in, preferred_element_type=F32)

    @pl.when(jnp.logical_not(at_top))
    def _():
        spread()

    if sections > 1:
        @pl.when(below_top)
        def _():
            pl.semaphore_wait(go_sem.at[1], 1)
            for o in range(nd):
                block = lax.rem(d + nd - o, nd)
                for oz in range(1, nz):
                    p_copy(oz, block).start()

    table_out = sign_rows(seed_ref[0, 1], d_start, cols, scale)

    def gp_copy(o, block):
        to = lax.rem(z + o, nz)
        return remote(
            gp_buf.at[z, block], gp_buf.at[z, block], gp_ss.at[o, block], gp_rs.at[o, block],
            dev(s, d, to),
        )

    for o in range(nd):
        block = lax.rem(d + nd - o, nd)
        summed = ps_buf[z, block].astype(F32)
        for oz in range(1, nz):
            p_copy(oz, block).wait_recv()
            summed = summed + pr_buf[lax.rem(z + nz - oz, nz), block].astype(F32)
        sig = jax.nn.sigmoid(summed)
        slope = sig * (1.0 + summed * (1.0 - sig))
        sum_buf[block] = summed
        slope_buf[block] = slope

        @pl.when(at_top)
        def _():
            if o:
                og_copy(o).wait_recv()
            else:
                ui_load().wait()
            gp_buf[z, block] = (ui_buf[block].astype(F32) * slope).astype(BF16)
            if sections > 1:
                for oz in range(1, nz):
                    gp_copy(oz, block).start()

    def up_copy(zt, source):
        return remote(
            up_buf.at[pl.ds(zt * sub, sub)], ui_buf.at[source], up_ss.at[zt], up_rs.at[source],
            dev(jnp.maximum(s - 1, 0), z, zt),
        )

    def uii_copy():
        return remote(up_buf, uii_buf, uii_ss.at[0], uii_rs.at[0], dev(jnp.maximum(s - 1, 0), d, z))

    @pl.when(at_top)
    def _():
        uii_load().wait()
        spread()

    @pl.when(jnp.logical_not(at_top))
    def _():
        for source in range(nd):
            up_copy(0, source).wait_recv()
        gp_buf[z] = (ui_buf[...].astype(F32) * slope_buf[...]).astype(BF16)

        @pl.when(lower)
        def _():
            for block in range(nd):
                for oz in range(1, nz):
                    gp_copy(oz, block).start()

    pl.semaphore_wait(far_sem.at[0], column - 1)
    grad_pre = gp_buf[z]
    plane = nd * nz
    mine = d * nz + z

    def dt_copy(o):
        to = lax.rem(mine + o, plane)
        return remote(
            dot_buf.at[mine], dot_buf.at[mine], dt_ss.at[o], dt_rs.at[o],
            dev(s, to // nz, lax.rem(to, nz)),
        )

    @pl.when(lower)
    def _():
        pre = gp_buf[z].astype(F32) * sum_buf[...]
        own_dot = jnp.sum(pre.reshape(nd * sub, cols), axis=1, keepdims=True)
        dot_buf[mine] = jnp.broadcast_to(own_dot, (tok, tok)).T[:8, :]
        for o in range(1, plane):
            dt_copy(o).start()

    out_feat = lax.dot_general(
        grad_pre.reshape(nd * sub, cols), table_out, NT, preferred_element_type=F32
    ).astype(BF16)
    for zt in range(nz):
        product = left_buf[zt] * jnp.dot(out_feat, pick_buf[zt], preferred_element_type=F32)
        for k in range(SEQS):
            g_buf[zt, k : k + 1, :] = jnp.sum(
                product[k * per_seq : (k + 1) * per_seq], axis=0, keepdims=True
            )

    def g_copy(o):
        to = lax.rem(mine + o, plane)
        return remote(
            g_buf.at[lax.rem(to, nz)], gr_buf.at[mine], g_ss.at[o], g_rs.at[o],
            dev(s, to // nz, lax.rem(to, nz)),
        )

    for o in range(1, plane):
        g_copy(o).start()
    gr_buf[mine] = g_buf[z]

    def gn_copy(o):
        to = lax.rem(d + nd - o, nd)
        return remote(gns_buf.at[to], gnr_buf.at[d], gn_ss.at[o], gn_rs.at[o], dev(s, to, z))

    @pl.when(lower)
    def _():
        for o in range(nd):
            block = lax.rem(d + nd - o, nd)
            for oz in range(1, nz):
                gp_copy(oz, block).wait_recv()
            if o == nd - 1:
                for each in range(nd):
                    for oz in range(1, nz):
                        gp_copy(oz, each).wait_send()

                @pl.when(at_top)
                def _():
                    go(1)

            rows = gp_buf[:, block].reshape(tok, cols)
            part = lax.dot_general(rows, w_ref[...], NT, preferred_element_type=F32).astype(BF16)
            if o:
                gns_buf[block] = part
                gn_copy(o).start()
            else:
                gnr_buf[d] = part
        for o in range(1, plane):
            dt_copy(o).wait_recv()
        for zt in range(nz):
            dots = dot_buf[zt]
            for dt in range(1, nd):
                dots = dots + dot_buf[dt * nz + zt]
            turn_buf[...] = jnp.broadcast_to(dots[:1, :] * (1.0 / width), (tok, tok)).T
            mean_buf[zt] = turn_buf[pl.ds(sub_start_d, sub), :]
        for o in range(1, nd):
            gn_copy(o).wait_recv()
        if sections > 2:
            @pl.when(jnp.logical_not(at_top))
            def _():
                uii_copy().wait_recv()
        for zt in range(nz):
            rows = pl.ds(zt * sub, sub)
            grad_norm = gnr_buf[0, rows].astype(F32)
            for dt in range(1, nd):
                grad_norm = grad_norm + gnr_buf[dt, rows].astype(F32)
            scaled = grad_norm.astype(BF16).astype(F32) * gain_ref[:, pl.ds(z_start, feat)]
            change = (scaled - norm_buf[rows] * mean_buf[zt][:, :1]) / rad_buf[rows, :1]
            up_buf[rows] = (uii_buf[rows].astype(F32) + change).astype(BF16)
            up_copy(zt, d).start()
        if sections > 2:
            @pl.when(s > 1)
            def _():
                uii_copy().start()

    for o in range(1, plane):
        g_copy(o).wait_recv()
    grads = gr_buf[0]
    for other in range(1, plane):
        grads = grads + gr_buf[other]
    out_ref[:, :piece] = grads
    queries = q_ref[...]
    high = grads.astype(BF16)
    rest = grads - high.astype(F32)
    middle = rest.astype(BF16)
    low = (rest - middle.astype(F32)).astype(BF16)
    part = lax.dot_general(high, queries, NT, preferred_element_type=F32)
    part = part + lax.dot_general(middle, queries, NT, preferred_element_type=F32)
    part = part + lax.dot_general(low, queries, NT, preferred_element_type=F32)
    sc_buf[here] = part

    def sc_copy(o):
        to = lax.rem(here + o, column)
        return remote(
            sc_buf.at[here], sc_buf.at[here], sc_ss.at[o], sc_rs.at[o],
            dev(to // nz, d, lax.rem(to, nz)),
        )

    for o in range(1, column):
        sc_copy(o).start()

    for o in range(1, nd):
        inf_copy(o).wait_send()
    for block in range(nd):
        for oz in range(1, nz):
            p_copy(oz, block).wait_send()

    @pl.when(at_top)
    def _():
        for o in range(1, nd):
            og_copy(o).wait_send()

    @pl.when(lower)
    def _():
        for o in range(1, plane):
            dt_copy(o).wait_send()
        for o in range(1, nd):
            gn_copy(o).wait_send()
        for zt in range(nz):
            up_copy(zt, d).wait_send()
        if sections > 2:
            @pl.when(s > 1)
            def _():
                uii_copy().wait_send()

    for o in range(1, plane):
        g_copy(o).wait_send()
    for o in range(1, column):
        sc_copy(o).wait_recv()
    scores = sc_buf[0]
    for other in range(1, column):
        scores = scores + sc_buf[other]
    out_ref[:, piece : piece + scores.shape[1]] = scores
    for o in range(1, column):
        sc_copy(o).wait_send()


def part_outputs(both_ref, grads_ref, scores_ref):
    piece = grads_ref.shape[1]
    grads_ref[...] = both_ref[:, :piece]
    scores_ref[...] = both_ref[:, piece : piece + scores_ref.shape[1]]


def body(section_input, weights, gains, proj_seeds, out_grad, query_grads):
    sections = lax.axis_size("section")
    nd = lax.axis_size("dp")
    nz = lax.axis_size("tensor")
    tok, width = section_input.shape[1:]
    feat = weights.shape[1]
    cols = weights.shape[2]
    assert nd == nz and feat == cols
    sub = tok // nz
    piece = R * R // nz
    queries = query_grads.shape[1]
    column = sections * nz
    plane = nd * nz
    vmem = pl.BlockSpec(memory_space=pltpu.VMEM)
    hbm = pl.BlockSpec(memory_space=pl.ANY)
    dma = pltpu.SemaphoreType.DMA
    sems = []
    for shape in ((nd,), (nd,), (nz, nd), (nd,), (nz, nd), (nd,), (plane,)):
        sems += [dma(shape), dma(shape)]
    sems += [dma((nz,)), dma((nd,)), dma((1,)), dma((1,))]
    sems += [dma((plane,)), dma((plane,)), dma((column,)), dma((column,))]
    out = pl.pallas_call(
        functools.partial(kernel, sections, nd, nz),
        out_shape=jax.ShapeDtypeStruct((SEQS, piece + queries), F32),
        in_specs=[hbm, hbm, vmem, pl.BlockSpec(memory_space=pltpu.SMEM), hbm, vmem],
        out_specs=vmem,
        scratch_shapes=[
            pltpu.VMEM((nd, tok, feat), BF16),
            pltpu.VMEM((nd, sub, R), F32),
            pltpu.VMEM((nz, nd, sub, cols), BF16),
            pltpu.VMEM((nz, nd, sub, cols), BF16),
            pltpu.VMEM((nd, sub, cols), F32),
            pltpu.VMEM((nd, sub, cols), BF16),
            pltpu.VMEM((tok, feat), BF16),
            pltpu.VMEM((nz, nd, sub, cols), BF16),
            pltpu.VMEM((nd, tok, feat), BF16),
            pltpu.VMEM((nd, tok, feat), BF16),
            pltpu.VMEM((plane, 8, tok), F32),
            pltpu.VMEM((tok, feat), BF16),
            pltpu.VMEM((nz, SEQS, piece), F32),
            pltpu.VMEM((plane, SEQS, piece), F32),
            pltpu.VMEM((column, SEQS, queries), F32),
            pltpu.VMEM((tok, width), BF16),
            pltpu.VMEM((feat, cols), BF16),
            pltpu.VMEM((nd, sub, cols), F32),
            pltpu.VMEM((tok, feat), F32),
            pltpu.VMEM((tok, 128), F32),
            pltpu.VMEM((tok, tok), F32),
            pltpu.VMEM((nz, sub, tok), F32),
            pltpu.VMEM((nz, tok, piece), F32),
            pltpu.VMEM((nz, R, piece), BF16),
            *sems,
            dma((4,)),
            pltpu.SemaphoreType.REGULAR((2,)),
            pltpu.SemaphoreType.REGULAR((1,)),
        ],
        compiler_params=pltpu.CompilerParams(
            collective_id=0, has_side_effects=True, vmem_limit_bytes=60 * 1024 * 1024
        ),
    )(section_input[0], weights[0], gains, proj_seeds, out_grad, query_grads[0])
    grads, scores = pl.pallas_call(
        part_outputs,
        out_shape=(
            jax.ShapeDtypeStruct((SEQS, piece), F32),
            jax.ShapeDtypeStruct((SEQS, queries), F32),
        ),
        in_specs=[vmem],
        out_specs=(vmem, vmem),
    )(out)
    return (grads[None], scores)


def solution(mesh):
    in_specs = (
        P("section", "dp", None),
        P("section", "tensor", "dp"),
        P("section", None),
        P("section", None),
        P("dp", None),
        P("section", "dp", "tensor"),
    )
    out_specs = (P("section", None, "tensor"), P(None, "dp"))
    return jax.shard_map(body, mesh=mesh, in_specs=in_specs, out_specs=out_specs, check_vma=False)
```

profile of v0, /device:TPU:0, one launch (start us, length us, event | category | flops | bytes accessed | tf_op | source)
XLA Modules:
  0.0 63.8 jit_solution(13706133538722792688)
XLA Ops:
  0.6 61.8 %shard_map.77.both_ref = f32[2,1088]{1,0:T(2,128)} custom-call(bf16[128,4096]{1,0:T(8,128)(2,1)} %bitcast.5, bf16[1024,1024]{1,0:T(8,128)(2,1)} %bitcast.4, f32[1,4096]{1,0:T(1,128)} %gain_ref.1, s32[1,2]{1,0:T(1,128)} %seed_ref.1, bf16[128,4096]{1,0:T(8,128)(2,1)} %og_ref.1, bf16[64,1024]{1,0:T(8,128)(2,1)} %bitcast.6), custom_call_target="tpu_custom_call" | custom-call | tf_op jit(solution)/shard_map/pallas_call | solution.py:452
  62.4 1.3 %shard_map.78 = (f32[2,1024]{1,0:T(2,128)}, f32[2,64]{1,0:T(2,128)}) custom-call(f32[2,1088]{1,0:T(2,128)} %shard_map.77.both_ref), custom_call_target="tpu_custom_call" | custom-call | tf_op jit(solution)/shard_map/pallas_call | solution.py:491
where the time goes:
time: 64.1 us; the launch traced here: 63.8 us
  Pallas kernels  63.1 us (98%)
    pallas_call x1, Pallas kernels, body(): pl.pallas_call(functools.partial(kernel, sections, nd, nz), out_shape=jax...  61.8 us
    pallas_call x1, Pallas kernels, body(): pl.pallas_call(part_outputs, out_shape=(jax.ShapeDtypeStruct((SEQS, piece...  1.3 us

commit v1 on v0

--- a/solution.py
+++ b/solution.py
@@ -15,6 +15,9 @@
 BF16 = jnp.bfloat16
 MESH = pl.DeviceIdType.MESH
 NT = (((1,), (1,)), ((), ()))
+LAG = 3
+GAP = 2
+LATE = 0
 
 
 def sign_rows(seed_value, row_start, row_count, scale):
@@ -422,23 +425,585 @@
         sc_copy(o).wait_send()
 
 
-def part_outputs(both_ref, grads_ref, scores_ref):
-    piece = grads_ref.shape[1]
-    grads_ref[...] = both_ref[:, :piece]
-    scores_ref[...] = both_ref[:, piece : piece + scores_ref.shape[1]]
-
-
-def body(section_input, weights, gains, proj_seeds, out_grad, query_grads):
-    sections = lax.axis_size("section")
-    nd = lax.axis_size("dp")
-    nz = lax.axis_size("tensor")
-    tok, width = section_input.shape[1:]
-    feat = weights.shape[1]
-    cols = weights.shape[2]
-    assert nd == nz and feat == cols
+def pair_kernel(
+    nd, nz, lag, gap, late,
+    x_hbm, w_hbm, gain_ref, seed_ref, og_ref, q_ref,
+    out_ref,
+    x_ref, w_ref, wide_ref, tab_in, tab_out, norm_buf, rad_buf,
+    a_buf, p_buf, un_buf, uo_buf, dn_buf, do_buf,
+    og_buf, uii_buf, gp_buf, dot_buf, gns_buf, gnr_buf, xs_buf, xr_buf,
+    so_buf, slope_buf, tabr_buf, infs_buf, infr_buf, low_buf,
+    left_buf, g_buf, gr_buf, g1_buf, gr1_buf, sc_buf,
+    in_sem, go_sem, far_sem,
+    a_ss, a_rs, og_ss, og_rs, up_ss, up_rs, dn_ss, dn_rs, gn_ss, gn_rs, xs_ss, xs_rs,
+    so_ss, so_rs, side_ss, side_rs, g_ss, g_rs, g1_ss, g1_rs, sc_ss, sc_rs,
+):
+    s = lax.axis_index("section")
+    d = lax.axis_index("dp")
+    z = lax.axis_index("tensor")
+    tok, width = x_hbm.shape
+    feat = width // nz
+    cols = width // nd
+    sub = tok // nz
+    plane = nd * nz
+    column = 2 * nz
+    piece = R * R // nz
+    lanes = tab_out.shape[0]
+    half = tok // 2
+    per_seq = nd // SEQS
+    at_top = s == 1
+    z_start = pl.multiple_of(z * feat, feat)
+    d_start = pl.multiple_of(d * cols, cols)
+    here = s * nz + z
+    mine = d * nz + z
+    scale = 1.0 / math.sqrt(width)
+
+    def dev(s_to, d_to, z_to):
+        return {"section": s_to, "dp": d_to, "tensor": z_to}
+
+    def flip(j):
+        to, bit = d, 1
+        while bit < nd:
+            flag = (j // bit) % 2 if isinstance(j, int) else lax.rem(lax.div(j, bit), 2)
+            to = to + flag * bit * (1 - 2 * lax.rem(lax.div(d, bit), 2))
+            bit *= 2
+        return to
+
+    def remote(src, dst, ss, rs, to):
+        return pltpu.make_async_remote_copy(
+            src_ref=src, dst_ref=dst, send_sem=ss, recv_sem=rs, device_id=to, device_id_type=MESH
+        )
+
+    def signal(sem, to):
+        pl.semaphore_signal(sem, inc=1, device_id=to, device_id_type=MESH)
+
+    x_load = pltpu.make_async_copy(x_hbm, x_ref, in_sem.at[0])
+    w_load = pltpu.make_async_copy(w_hbm, w_ref, in_sem.at[1])
+    x_load.start()
+    w_load.start()
+    barrier = pltpu.get_barrier_semaphore()
+
+    def signal_column(sem):
+        for o in range(1, column):
+            to = lax.rem(here + o, column)
+            signal(sem, dev(to // nz, d, lax.rem(to, nz)))
+
+    for j in range(1, nd):
+        signal(barrier, dev(s, flip(j), z))
+    signal_column(barrier)
+
+    ui_load = pltpu.make_async_copy(og_ref.at[:, pl.ds(d_start, cols)], og_buf.at[0], in_sem.at[2])
+    uii_load = pltpu.make_async_copy(og_ref.at[:, pl.ds(z_start, feat)], uii_buf, in_sem.at[3])
+
+    @pl.when(at_top)
+    def _():
+        ui_load.start()
+        uii_load.start()
+
+    table_row = jnp.where(at_top, d_start, z_start)
+    tab_out[:R] = sign_rows(seed_ref[0, 1], table_row, cols, scale)
+    tab_out[R:] = jnp.zeros((lanes - R, cols), BF16)
+    tab_in[...] = sign_rows(seed_ref[0, 0], 0, width, scale)
+
+    x_load.wait()
+    hidden = x_ref[...].astype(F32)
+    radius = jnp.sqrt(jnp.mean(hidden * hidden, axis=1, keepdims=True) + eps)
+    normed_z = x_ref[:, pl.ds(z_start, feat)].astype(F32) / radius
+    norm_buf[...] = normed_z
+    rad_buf[...] = jnp.broadcast_to(radius, rad_buf.shape)
+    a_buf[0] = (normed_z * gain_ref[:, pl.ds(z_start, feat)]).astype(BF16)
+
+    pl.semaphore_wait(barrier, nd - 1 + column - 1)
+
+    def a_copy(j, h, via=0):
+        rows = pl.ds(h * half, half)
+        return remote(
+            a_buf.at[via, rows], a_buf.at[j, rows], a_ss.at[j, h], a_rs.at[j, h], dev(s, flip(j - via), z)
+        )
+
+    def a_start():
+        a_copy(1, 0).start()
+        a_copy(2, 1).start()
+        a_copy(1, 1).start()
+        a_copy(2, 0).start()
+
+    def a_wait(j):
+        if j == 1:
+            a_copy(1, 0).wait_recv()
+            a_copy(3, 0, 1).start()
+            a_copy(2, 1).wait_recv()
+            a_copy(3, 1, 2).start()
+            a_copy(1, 1).wait_recv()
+        if j == 2:
+            a_copy(2, 0).wait_recv()
+        if j == 3:
+            for h in range(2):
+                a_copy(3, h).wait_recv()
+
+    def a_sent():
+        for j in range(1, nd):
+            for h in range(2):
+                a_copy(j, h).wait_send()
+
+    def og_copy(j):
+        to = flip(j)
+        src = og_ref.at[:, pl.ds(pl.multiple_of(to * cols, cols), cols)]
+        return remote(src, og_buf.at[j], og_ss.at[j], og_rs.at[j], dev(s, to, z))
+
+    @pl.when(at_top)
+    def _():
+        a_start()
+        og_copy(1).start()
+        og_copy(2).start()
+
+    signal_column(far_sem.at[0])
+    w_load.wait()
+
+    def in_features():
+        lifted = (x_ref[...].astype(F32) / rad_buf[:, :1] * gain_ref[...]).astype(BF16)
+        return lax.dot_general(lifted, tab_in[...], NT, preferred_element_type=F32).astype(BF16)
+
+    def pick_in(zt):
+        entry = lax.broadcasted_iota(jnp.int32, (R, piece), 1) + zt * piece
+        which = lax.broadcasted_iota(jnp.int32, (R, piece), 0)
+        return (entry // R == which).astype(F32).astype(BF16)
+
+    def pick_out():
+        entry = lax.broadcasted_iota(jnp.int32, (R, piece), 1)
+        which = lax.broadcasted_iota(jnp.int32, (R, piece), 0)
+        return (entry % R == which).astype(F32).astype(BF16)
+
+    def up_copy(c, first):
+        src = p_buf.at[c] if first else uo_buf.at[c]
+        return remote(src, un_buf.at[c], up_ss.at[c], up_rs.at[c], dev(s, d, jnp.minimum(z + 1, nz - 1)))
+
+    def dn_copy(c, first):
+        src = p_buf.at[c] if first else do_buf.at[c]
+        return remote(src, dn_buf.at[c], dn_ss.at[c], dn_rs.at[c], dev(s, d, jnp.maximum(z - 1, 0)))
+
+    def gn_copy(j, row, rows, h, to):
+        return remote(
+            gns_buf.at[j, pl.ds(row, rows)], gnr_buf.at[j, pl.ds(row, rows)],
+            gn_ss.at[j, h], gn_rs.at[j, h], dev(s, to, z),
+        )
+
+    def xs_copy(j, row, rows, h, to):
+        return remote(
+            xs_buf.at[j, pl.ds(row, rows)], xr_buf.at[j, pl.ds(row, rows)],
+            xs_ss.at[j, h], xs_rs.at[j, h], dev(s, to, z),
+        )
+
+    def so_copy(j, to):
+        return remote(so_buf.at[j], slope_buf.at[z], so_ss.at[j], so_rs.at[z], dev(1, to, d))
+
+    def so_arrival(k):
+        return remote(so_buf.at[0], slope_buf.at[k], so_ss.at[0], so_rs.at[k], dev(0, d, z))
+
+    def back(j, row, rows):
+        pre = gp_buf[j, pl.ds(row, rows)]
+        both = jnp.dot(pre, wide_ref[...], preferred_element_type=F32)
+        dot = dot_buf[j, pl.ds(row, rows)]
+        high = dot.astype(BF16).astype(F32)
+        lane = lax.broadcasted_iota(jnp.int32, (rows, lanes), 1)
+        extra = jnp.where(lane == R, high, jnp.where(lane == R + 1, dot - high, both[:, feat:]))
+        return both[:, :feat].astype(BF16), extra.astype(BF16)
+
+    def slope_of(total):
+        sig = jax.nn.sigmoid(total)
+        return sig * (1.0 + total * (1.0 - sig))
+
+    lag_up = z * lag
+    lag_dn = (nz - 1 - z) * lag
+    lag_all = jnp.maximum(lag_up, lag_dn) + late
+    slots = plane + gap + (nz - 1) * lag + late
+
+    def chunk_at(v):
+        valid = jnp.logical_and(v >= 0, v < plane + gap)
+        valid = jnp.logical_and(valid, jnp.logical_or(v < nz, v >= nz + gap))
+        return jnp.where(v < nz, v, v - gap), valid
+
+    def relay(c, valid, gets, sends, copy, inbox, outbox):
+
+        @pl.when(jnp.logical_and(valid, gets))
+        def _():
+            copy(c, True).wait_recv()
+
+        @pl.when(jnp.logical_and(valid, jnp.logical_and(sends, jnp.logical_not(gets))))
+        def _():
+            copy(c, True).start()
+
+        @pl.when(jnp.logical_and(valid, jnp.logical_and(sends, gets)))
+        def _():
+            outbox[c] = (inbox[c].astype(F32) + p_buf[c].astype(F32)).astype(BF16)
+            copy(c, False).start()
+
+    def sweep(on_block, on_total):
+        def slot(i, carry):
+            for j in range(nd):
+                @pl.when(i == (j * nz + gap if j else 0))
+                def _(j=j):
+                    on_block(j)
+                    multiply(j)
+
+            c, valid = chunk_at(i - lag_up)
+            relay(c, valid, z > 0, z < nz - 1, up_copy, un_buf, uo_buf)
+            c, valid = chunk_at(i - lag_dn)
+            relay(c, valid, z < nz - 1, z > 0, dn_copy, dn_buf, do_buf)
+            c, valid = chunk_at(i - lag_all)
+            q = lax.rem(jnp.maximum(c, 0), nz)
+            j_now = lax.div(jnp.maximum(c, 0), nz)
+
+            def total_of(up, dn):
+                total = p_buf[c].astype(F32)
+                if up:
+                    total = total + un_buf[c].astype(F32)
+                if dn:
+                    total = total + dn_buf[c].astype(F32)
+                on_total(j_now, q, total)
+
+            @pl.when(jnp.logical_and(valid, z == 0))
+            def _():
+                total_of(False, True)
+
+            @pl.when(jnp.logical_and(valid, z == nz - 1))
+            def _():
+                total_of(True, False)
+
+            @pl.when(jnp.logical_and(valid, jnp.logical_and(z > 0, z < nz - 1)))
+            def _():
+                total_of(True, True)
+
+            @pl.when(valid)
+            def _():
+                after_total(j_now, q)
+
+            return carry
+
+        lax.fori_loop(0, slots, slot, 0)
+
+    def multiply(j):
+        part = jnp.dot(a_buf[j], w_ref[...], preferred_element_type=F32).astype(BF16)
+        for q in range(nz):
+            p_buf[j * nz + q] = part[q * sub : (q + 1) * sub]
+
+    def after_total(j, q):
+        @pl.when(jnp.logical_and(q == nz - 1, j == 0))
+        def _():
+            gnr_buf[0], xr_buf[0] = back(0, 0, tok)
+
+        @pl.when(jnp.logical_and(q == nz - 1, jnp.logical_and(j > 0, j < nd - 1)))
+        def _():
+            gns_buf[j], xs_buf[j] = back(j, 0, tok)
+            gn_copy(j, 0, tok, 0, flip(j)).start()
+            xs_copy(j, 0, tok, 0, flip(j)).start()
+
+        for h in range(2):
+            @pl.when(jnp.logical_and(q == (h + 1) * nz // 2 - 1, j == nd - 1))
+            def _(h=h):
+                last, rows = nd - 1, pl.ds(h * half, half)
+                gns_buf[last, rows], xs_buf[last, rows] = back(last, h * half, half)
+                gn_copy(last, h * half, half, h, flip(last)).start()
+                xs_copy(last, h * half, half, h, flip(last)).start()
+
+    def sweep_sent():
+        def one(c, carry):
+            @pl.when(z < nz - 1)
+            def _():
+                up_copy(c, True).wait_send()
+
+            @pl.when(z > 0)
+            def _():
+                dn_copy(c, True).wait_send()
+
+            return carry
+
+        lax.fori_loop(0, plane, one, 0)
+
+    def g_copy(o):
+        return remote(g_buf.at[o % nz], gr_buf.at[mine], g_ss.at[o], g_rs.at[mine], dev(0, o // nz, o % nz))
+
+    def g_arrival(o):
+        return remote(g_buf.at[0], gr_buf.at[o], g_ss.at[o], g_rs.at[o], dev(1, d, z))
+
+    def g1_copy(j):
+        return remote(g1_buf, gr1_buf.at[j], g1_ss.at[j], g1_rs.at[j], dev(1, flip(j), z))
+
+    def side_copy(which):
+        src, dst = ((infs_buf, infr_buf), (tab_out, tabr_buf))[which]
+        return remote(src, dst, side_ss.at[which], side_rs.at[which], dev(1, d, z))
+
+    def side_arrival(which):
+        src, dst = ((infs_buf, infr_buf), (tab_out, tabr_buf))[which]
+        return remote(src, dst, side_ss.at[which], side_rs.at[which], dev(0, d, z))
+
+    def sc_copy(o):
+        to = lax.rem(here + o, column)
+        return remote(
+            sc_buf.at[here], sc_buf.at[here], sc_ss.at[o], sc_rs.at[o], dev(to // nz, d, lax.rem(to, nz))
+        )
+
+    def score():
+        grads = out_ref[:, :piece]
+        queries = q_ref[...]
+        high = grads.astype(BF16)
+        rest = grads - high.astype(F32)
+        middle = rest.astype(BF16)
+        low = (rest - middle.astype(F32)).astype(BF16)
+        part = lax.dot_general(high, queries, NT, preferred_element_type=F32)
+        part = part + lax.dot_general(middle, queries, NT, preferred_element_type=F32)
+        part = part + lax.dot_general(low, queries, NT, preferred_element_type=F32)
+        sc_buf[here] = part
+        for o in range(1, column):
+            sc_copy(o).start()
+
+    @pl.when(at_top)
+    def _():
+        def on_block(j):
+            if j == 1:
+                wide_ref[:, :feat] = w_ref[...].T
+                wide_ref[:, feat:] = tab_out[...].T
+            a_wait(j)
+            if j == 1:
+                signal(go_sem.at[0], dev(0, d, z))
+            if j == 2:
+                og_copy(3).start()
+
+        def on_total(j, q, total):
+            for each in range(nd):
+                @pl.when(jnp.logical_and(q == 0, j == each))
+                def _(each=each):
+                    if each:
+                        og_copy(each).wait_recv()
+                    else:
+                        ui_load.wait()
+
+            rows = pl.ds(pl.multiple_of(q * sub, sub), sub)
+            pre = (og_buf[j, rows].astype(F32) * slope_of(total)).astype(BF16)
+            gp_buf[j, rows] = pre
+            dot = jnp.sum(pre.astype(F32) * total, axis=1, keepdims=True)
+            dot_buf[j, rows] = jnp.broadcast_to(dot, (sub, lanes))
+
+        sweep(on_block, on_total)
+
+        in_feat = in_features()
+        g_left = jnp.dot(in_feat, pick_in(z), preferred_element_type=F32)
+        left_buf[nz] = g_left
+        for which in range(2):
+            side_arrival(which).wait_recv()
+        for zt in range(nz):
+            left_buf[zt] = jnp.dot(infr_buf[:, :R], pick_in(zt), preferred_element_type=F32)
+        uii_load.wait()
+        pl.semaphore_wait(far_sem.at[0], column - 1)
+        for k in range(nz):
+            so_arrival(k).wait_recv()
+        for j in range(1, nd - 1):
+            gn_copy(j, 0, tok, 0, d).wait_recv()
+            xs_copy(j, 0, tok, 0, d).wait_recv()
+        for k in range(nz):
+            if k * 2 % nz == 0:
+                h = k * 2 // nz
+                gn_copy(nd - 1, h * half, half, h, d).wait_recv()
+                xs_copy(nd - 1, h * half, half, h, d).wait_recv()
+            rows = pl.ds(k * sub, sub)
+            grad_norm = gnr_buf[0, rows].astype(F32)
+            extra = xr_buf[0, rows].astype(F32)
+            for j in range(1, nd):
+                grad_norm = grad_norm + gnr_buf[j, rows].astype(F32)
+                extra = extra + xr_buf[j, rows].astype(F32)
+            dot_buf[0, rows] = extra
+            mean_dot = (extra[:, R : R + 1] + extra[:, R + 1 : R + 2]) * (1.0 / width)
+            scaled = grad_norm.astype(BF16).astype(F32) * gain_ref[:, pl.ds(z_start, feat)]
+            change = (scaled - norm_buf[rows] * mean_dot) / rad_buf[rows, :1]
+            upstream = (uii_buf[rows].astype(F32) + change).astype(BF16)
+            low_buf[rows] = (upstream.astype(F32) * slope_buf[k].astype(F32)).astype(BF16)
+        out_low = lax.dot_general(low_buf[...], tabr_buf[...], NT, preferred_element_type=F32)
+        spread = pick_out()
+        right = jnp.dot(out_low[:, :R].astype(BF16), spread, preferred_element_type=F32)
+        for zt in range(nz):
+            g_buf[zt] = jnp.sum(left_buf[zt] * right, axis=0, keepdims=True)
+        for o in range(plane):
+            g_copy(o).start()
+
+        right = jnp.dot(dot_buf[0, :, :R].astype(BF16), spread, preferred_element_type=F32)
+        own = jnp.sum(left_buf[nz] * right, axis=0, keepdims=True)
+        g1_buf[...] = own
+        for j in range(1, nd):
+            g1_copy(j).start()
+        gr1_buf[0] = own
+        for j in range(1, nd):
+            g1_copy(j).wait_recv()
+        for k in range(SEQS):
+            row = jnp.zeros((1, piece), F32)
+            for group in range(SEQS):
+                held = gr1_buf[group * per_seq]
+                for j in range(group * per_seq + 1, (group + 1) * per_seq):
+                    held = held + gr1_buf[j]
+                row = row + jnp.where(lax.div(flip(group * per_seq), per_seq) == k, held, 0.0)
+            out_ref[k : k + 1, :piece] = row
+        score()
+        for j in range(1, nd):
+            og_copy(j).wait_send()
+            g1_copy(j).wait_send()
+        for j in range(1, nd - 1):
+            gn_copy(j, 0, tok, 0, d).wait_send()
+            xs_copy(j, 0, tok, 0, d).wait_send()
+        for h in range(2):
+            gn_copy(nd - 1, h * half, half, h, d).wait_send()
+            xs_copy(nd - 1, h * half, half, h, d).wait_send()
+        for o in range(plane):
+            g_copy(o).wait_send()
+        a_sent()
+        sweep_sent()
+
+    @pl.when(jnp.logical_not(at_top))
+    def _():
+        def chain_up(block, valid):
+            for q in reversed(range(nz)):
+                relay(
+                    block * nz + q, valid, jnp.logical_and(z > 0, q >= z), q > z, up_copy, un_buf, uo_buf
+                )
+
+        def chain_dn(block, valid):
+            for q in range(nz):
+                relay(
+                    block * nz + q, valid, jnp.logical_and(z < nz - 1, q <= z), q < z, dn_copy, dn_buf, do_buf
+                )
+
+        def lower_slope(block):
+            c = block * nz + z
+            total = p_buf[c].astype(F32)
+            total = total + jnp.where(z > 0, un_buf[c].astype(F32), 0.0)
+            total = total + jnp.where(z < nz - 1, dn_buf[c].astype(F32), 0.0)
+            so_buf[block] = slope_of(total).astype(BF16)
+            so_copy(block, flip(block)).start()
+
+        far_end = jnp.maximum(z, nz - 1 - z)
+        multiply(0)
+        chain_up(0, z == 0)
+        chain_dn(0, z == nz - 1)
+        infs_buf[:, :R] = in_features()
+        infs_buf[:, R:] = jnp.zeros((tok, lanes - R), BF16)
+        for which in range(2):
+            side_copy(which).start()
+        pl.semaphore_wait(go_sem.at[0], 1)
+        a_start()
+        pl.semaphore_wait(far_sem.at[0], column - 1)
+        for hop in range(1, nz):
+            chain_up(0, z == hop)
+            chain_dn(0, nz - 1 - z == hop)
+        lower_slope(0)
+        for block in range(1, nd):
+            a_wait(block)
+            multiply(block)
+            chain_up(block, z == 0)
+            chain_dn(block, z == nz - 1)
+        for step in range(1, nd + nz - 2):
+            block = step + 1 - z
+            chain_up(block, jnp.logical_and(z > 0, jnp.logical_and(block >= 1, block < nd)))
+            block = step + 2 - nz + z
+            chain_dn(block, jnp.logical_and(z < nz - 1, jnp.logical_and(block >= 1, block < nd)))
+            block = step + 1 - far_end
+
+            @pl.when(jnp.logical_and(block >= 1, block < nd))
+            def _(block=block):
+                lower_slope(block)
+
+        for o in range(plane):
+            g_arrival(o).wait_recv()
+        for k in range(SEQS):
+            held = gr_buf[k * per_seq * nz]
+            for o in range(k * per_seq * nz + 1, (k + 1) * per_seq * nz):
+                held = held + gr_buf[o]
+            out_ref[k : k + 1, :piece] = held
+        score()
+        a_sent()
+        for j in range(nd):
+            so_copy(j, d).wait_send()
+        for which in range(2):
+            side_copy(which).wait_send()
+        for j in range(nd):
+            for q in range(nz):
+                @pl.when(q > z)
+                def _(c=j * nz + q):
+                    up_copy(c, True).wait_send()
+
+                @pl.when(q < z)
+                def _(c=j * nz + q):
+                    dn_copy(c, True).wait_send()
+
+    for o in range(1, column):
+        sc_copy(o).wait_recv()
+    scores = sc_buf[0]
+    for other in range(1, column):
+        scores = scores + sc_buf[other]
+    out_ref[:, piece : piece + scores.shape[1]] = scores
+    for o in range(1, column):
+        sc_copy(o).wait_send()
+
+
+def pair_call(nd, nz, tok, width, queries):
+    feat, cols, sub, plane, column = width // nz, width // nd, tok // nz, nd * nz, 2 * nz
+    piece, lanes = R * R // nz, 2 * R
+    dma = pltpu.SemaphoreType.DMA
+    sems = []
+    for shape in (
+        (nd, 2), (nd,), (plane,), (plane,), (nd, 2), (nd, 2),
+    ):
+        sems += [dma(shape), dma(shape)]
+    sems += [dma((nd,)), dma((nz,)), dma((2,)), dma((2,)), dma((plane,)), dma((plane,))]
+    sems += [dma((nd,)), dma((nd,)), dma((column,)), dma((column,))]
+    vmem = pl.BlockSpec(memory_space=pltpu.VMEM)
+    hbm = pl.BlockSpec(memory_space=pl.ANY)
+    chunks = pltpu.VMEM((plane, sub, cols), BF16)
+    blocks = pltpu.VMEM((nd, tok, cols), BF16)
+    return pl.pallas_call(
+        functools.partial(pair_kernel, nd, nz, LAG, GAP, LATE),
+        out_shape=pltpu.VMEM((SEQS, piece + queries), F32),
+        in_specs=[hbm, hbm, vmem, pl.BlockSpec(memory_space=pltpu.SMEM), hbm, vmem],
+        out_specs=vmem,
+        scratch_shapes=[
+            pltpu.VMEM((tok, width), BF16),
+            pltpu.VMEM((feat, cols), BF16),
+            pltpu.VMEM((cols, feat + lanes), BF16),
+            pltpu.VMEM((R, width), BF16),
+            pltpu.VMEM((lanes, cols), BF16),
+            pltpu.VMEM((tok, feat), F32),
+            pltpu.VMEM((tok, 128), F32),
+            blocks, chunks, chunks, chunks, chunks, chunks,
+            blocks,
+            pltpu.VMEM((tok, feat), BF16),
+            blocks,
+            pltpu.VMEM((nd, tok, lanes), F32),
+            blocks, blocks,
+            pltpu.VMEM((nd, tok, lanes), BF16),
+            pltpu.VMEM((nd, tok, lanes), BF16),
+            pltpu.VMEM((nd, sub, cols), BF16),
+            pltpu.VMEM((nz, sub, cols), BF16),
+            pltpu.VMEM((lanes, cols), BF16),
+            pltpu.VMEM((tok, lanes), BF16),
+            pltpu.VMEM((tok, lanes), BF16),
+            pltpu.VMEM((tok, cols), BF16),
+            pltpu.VMEM((nz + 1, tok, piece), F32),
+            pltpu.VMEM((nz, 1, piece), F32),
+            pltpu.VMEM((plane, 1, piece), F32),
+            pltpu.VMEM((1, piece), F32),
+            pltpu.VMEM((nd, 1, piece), F32),
+            pltpu.VMEM((column, SEQS, queries), F32),
+            dma((4,)),
+            pltpu.SemaphoreType.REGULAR((2,)),
+            pltpu.SemaphoreType.REGULAR((1,)),
+            *sems,
+        ],
+        compiler_params=pltpu.CompilerParams(
+            collective_id=0, has_side_effects=True, vmem_limit_bytes=60 * 1024 * 1024
+        ),
+    )
+
+
+def stack_call(sections, nd, nz, tok, width, queries):
+    feat, cols = width // nz, width // nd
     sub = tok // nz
     piece = R * R // nz
-    queries = query_grads.shape[1]
     column = sections * nz
     plane = nd * nz
     vmem = pl.BlockSpec(memory_space=pltpu.VMEM)
@@ -449,7 +1014,7 @@
         sems += [dma(shape), dma(shape)]
     sems += [dma((nz,)), dma((nd,)), dma((1,)), dma((1,))]
     sems += [dma((plane,)), dma((plane,)), dma((column,)), dma((column,))]
-    out = pl.pallas_call(
+    return pl.pallas_call(
         functools.partial(kernel, sections, nd, nz),
         out_shape=jax.ShapeDtypeStruct((SEQS, piece + queries), F32),
         in_specs=[hbm, hbm, vmem, pl.BlockSpec(memory_space=pltpu.SMEM), hbm, vmem],
@@ -487,7 +1052,34 @@
         compiler_params=pltpu.CompilerParams(
             collective_id=0, has_side_effects=True, vmem_limit_bytes=60 * 1024 * 1024
         ),
-    )(section_input[0], weights[0], gains, proj_seeds, out_grad, query_grads[0])
+    )
+
+
+def part_outputs(both_ref, grads_ref, scores_ref):
+    piece = grads_ref.shape[1]
+    grads_ref[...] = both_ref[:, :piece]
+    scores_ref[...] = both_ref[:, piece : piece + scores_ref.shape[1]]
+
+
+def body(section_input, weights, gains, proj_seeds, out_grad, query_grads):
+    sections = lax.axis_size("section")
+    nd = lax.axis_size("dp")
+    nz = lax.axis_size("tensor")
+    tok, width = section_input.shape[1:]
+    feat = weights.shape[1]
+    cols = weights.shape[2]
+    assert nd == nz and feat == cols
+    piece = R * R // nz
+    queries = query_grads.shape[1]
+    vmem = pl.BlockSpec(memory_space=pltpu.VMEM)
+    paired = sections == 2 and nd == 4 and nz % 2 == 0
+    if paired:
+        call = pair_call(nd, nz, tok, width, queries)
+    else:
+        call = stack_call(sections, nd, nz, tok, width, queries)
+    out = call(section_input[0], weights[0], gains, proj_seeds, out_grad, query_grads[0])
+    if paired:
+        out = pltpu.with_memory_space_constraint(out, pltpu.VMEM)
     grads, scores = pl.pallas_call(
         part_outputs,
         out_shape=(

time: 64.1 us -> 56.3 us (0.88)
  Pallas kernels: 63.1 us -> 55.4 us
    pallas_call x1, Pallas kernels: 61.8 us -> 54.8 us  [body(): call(section_input[0], weights[0], gains, proj_seeds, out_grad, query_gra...]
    pallas_call x1, Pallas kernels: 1.3 us -> 0.6 us  [body(): pl.pallas_call(part_outputs, out_shape=(jax.ShapeDtypeStruct((SEQS, piece...]
where the time goes in v1:
time: 56.3 us; the launch traced here: 56.1 us
  Pallas kernels  55.4 us (98%)
  between operations  0.64 us (1%)
    pallas_call x1, Pallas kernels, body(): call(section_input[0], weights[0], gains, proj_seeds, out_grad, query_gra...  54.8 us

profile of v1, /device:TPU:0, one launch (start us, length us, event | category | flops | bytes accessed | tf_op | source)
XLA Modules:
  0.0 56.1 jit_solution(4897500113106253540)
XLA Ops:
  0.6 54.8 %shard_map.77.both_ref = f32[2,1088]{1,0:T(2,128)S(1)} custom-call(bf16[128,4096]{1,0:T(8,128)(2,1)} %bitcast.5, bf16[1024,1024]{1,0:T(8,128)(2,1)} %bitcast.4, f32[1,4096]{1,0:T(1,128)} %gain_ref.1, s32[1,2]{1,0:T(1,128)} %seed_ref.1, bf16[128,4096]{1,0:T(8,128)(2,1)} %og_ref.1, bf16[64,1024]{1,0:T(8,128)(2,1)} %bitcast.6), custom_call_target="tpu_custom_call" | custom-call | tf_op jit(solution)/shard_map/pallas_call | solution.py:1080
  55.5 0.6 %shard_map.78 = (f32[2,1024]{1,0:T(2,128)}, f32[2,64]{1,0:T(2,128)}) custom-call(f32[2,1088]{1,0:T(2,128)S(1)} %shard_map.77.both_ref), custom_call_target="tpu_custom_call" | custom-call | tf_op jit(solution)/shard_map/pallas_call | solution.py:1083

commit v2 on v1

--- a/solution.py
+++ b/solution.py
@@ -15,9 +15,11 @@
 BF16 = jnp.bfloat16
 MESH = pl.DeviceIdType.MESH
 NT = (((1,), (1,)), ((), ()))
-LAG = 3
-GAP = 2
+LAG = 6
+GAP = 3
 LATE = 0
+OGA = 1
+OGB = 2
 
 
 def sign_rows(seed_value, row_start, row_count, scale):
@@ -431,12 +433,12 @@
     out_ref,
     x_ref, w_ref, wide_ref, tab_in, tab_out, norm_buf, rad_buf,
     a_buf, p_buf, un_buf, uo_buf, dn_buf, do_buf,
-    og_buf, uii_buf, gp_buf, dot_buf, gns_buf, gnr_buf, xs_buf, xr_buf,
+    og_buf, uii_buf, gp_buf, dot_buf, gns_buf, gnr_buf,
     so_buf, slope_buf, tabr_buf, infs_buf, infr_buf, low_buf,
     left_buf, g_buf, gr_buf, g1_buf, gr1_buf, sc_buf,
     in_sem, go_sem, far_sem,
-    a_ss, a_rs, og_ss, og_rs, up_ss, up_rs, dn_ss, dn_rs, gn_ss, gn_rs, xs_ss, xs_rs,
-    so_ss, so_rs, side_ss, side_rs, g_ss, g_rs, g1_ss, g1_rs, sc_ss, sc_rs,
+    a_ss, a_rs, og_ss, og_rs, up_ss, up_rs, dn_ss, dn_rs, gn_ss, gn_rs,
+    so_ss, so_rs, sl_ss, sl_rs, side_ss, side_rs, g_ss, g_rs, g1_ss, g1_rs, sc_ss, sc_rs,
 ):
     s = lax.axis_index("section")
     d = lax.axis_index("dp")
@@ -518,7 +520,8 @@
     def a_copy(j, h, via=0):
         rows = pl.ds(h * half, half)
         return remote(
-            a_buf.at[via, rows], a_buf.at[j, rows], a_ss.at[j, h], a_rs.at[j, h], dev(s, flip(j - via), z)
+            a_buf.at[via, rows], a_buf.at[j, rows], a_ss.at[0], a_rs.at[2 * j + h - 2],
+            dev(s, flip(j - via), z),
         )
 
     def a_start():
@@ -541,20 +544,17 @@
                 a_copy(3, h).wait_recv()
 
     def a_sent():
-        for j in range(1, nd):
-            for h in range(2):
-                a_copy(j, h).wait_send()
+        moved = a_buf.at[pl.ds(1, nd - 1)]
+        remote(moved, moved, a_ss.at[0], a_rs.at[0], dev(s, flip(1), z)).wait_send()
 
     def og_copy(j):
         to = flip(j)
         src = og_ref.at[:, pl.ds(pl.multiple_of(to * cols, cols), cols)]
-        return remote(src, og_buf.at[j], og_ss.at[j], og_rs.at[j], dev(s, to, z))
+        return remote(src, og_buf.at[j], og_ss.at[0], og_rs.at[j - 1], dev(s, to, z))
 
     @pl.when(at_top)
     def _():
         a_start()
-        og_copy(1).start()
-        og_copy(2).start()
 
     signal_column(far_sem.at[0])
     w_load.wait()
@@ -575,38 +575,37 @@
 
     def up_copy(c, first):
         src = p_buf.at[c] if first else uo_buf.at[c]
-        return remote(src, un_buf.at[c], up_ss.at[c], up_rs.at[c], dev(s, d, jnp.minimum(z + 1, nz - 1)))
+        return remote(src, un_buf.at[c], up_ss.at[0], up_rs.at[c], dev(s, d, jnp.minimum(z + 1, nz - 1)))
 
     def dn_copy(c, first):
         src = p_buf.at[c] if first else do_buf.at[c]
-        return remote(src, dn_buf.at[c], dn_ss.at[c], dn_rs.at[c], dev(s, d, jnp.maximum(z - 1, 0)))
+        return remote(src, dn_buf.at[c], dn_ss.at[0], dn_rs.at[c], dev(s, d, jnp.maximum(z - 1, 0)))
 
     def gn_copy(j, row, rows, h, to):
         return remote(
             gns_buf.at[j, pl.ds(row, rows)], gnr_buf.at[j, pl.ds(row, rows)],
-            gn_ss.at[j, h], gn_rs.at[j, h], dev(s, to, z),
-        )
-
-    def xs_copy(j, row, rows, h, to):
-        return remote(
-            xs_buf.at[j, pl.ds(row, rows)], xr_buf.at[j, pl.ds(row, rows)],
-            xs_ss.at[j, h], xs_rs.at[j, h], dev(s, to, z),
-        )
-
-    def so_copy(j, to):
-        return remote(so_buf.at[j], slope_buf.at[z], so_ss.at[j], so_rs.at[z], dev(1, to, d))
-
-    def so_arrival(k):
-        return remote(so_buf.at[0], slope_buf.at[k], so_ss.at[0], so_rs.at[k], dev(0, d, z))
-
-    def back(j, row, rows):
+            gn_ss.at[0], gn_rs.at[j - 1 + h], dev(s, to, z),
+        )
+
+    def so_copy(j):
+        return remote(so_buf.at[0, j], so_buf.at[1, j], so_ss.at[0], so_rs.at[j - 1], dev(0, flip(j), z))
+
+    def slope_copy(j):
+        src = so_buf.at[1, j] if j else so_buf.at[0, 0]
+        return remote(src, slope_buf.at[z], sl_ss.at[0], sl_rs.at[0], dev(1, d, flip(j)))
+
+    def slope_arrival():
+        return remote(so_buf.at[0], slope_buf, sl_ss.at[0], sl_rs.at[0], dev(1 - s, d, z))
+
+    def back(buf, j, row, rows):
         pre = gp_buf[j, pl.ds(row, rows)]
         both = jnp.dot(pre, wide_ref[...], preferred_element_type=F32)
         dot = dot_buf[j, pl.ds(row, rows)]
         high = dot.astype(BF16).astype(F32)
         lane = lax.broadcasted_iota(jnp.int32, (rows, lanes), 1)
         extra = jnp.where(lane == R, high, jnp.where(lane == R + 1, dot - high, both[:, feat:]))
-        return both[:, :feat].astype(BF16), extra.astype(BF16)
+        buf[j, pl.ds(row, rows), :feat] = both[:, :feat].astype(BF16)
+        buf[j, pl.ds(row, rows), feat:] = extra.astype(BF16)
 
     def slope_of(total):
         sig = jax.nn.sigmoid(total)
@@ -689,44 +688,28 @@
     def after_total(j, q):
         @pl.when(jnp.logical_and(q == nz - 1, j == 0))
         def _():
-            gnr_buf[0], xr_buf[0] = back(0, 0, tok)
+            back(gnr_buf, 0, 0, tok)
 
         @pl.when(jnp.logical_and(q == nz - 1, jnp.logical_and(j > 0, j < nd - 1)))
         def _():
-            gns_buf[j], xs_buf[j] = back(j, 0, tok)
+            back(gns_buf, j, 0, tok)
             gn_copy(j, 0, tok, 0, flip(j)).start()
-            xs_copy(j, 0, tok, 0, flip(j)).start()
 
         for h in range(2):
             @pl.when(jnp.logical_and(q == (h + 1) * nz // 2 - 1, j == nd - 1))
             def _(h=h):
-                last, rows = nd - 1, pl.ds(h * half, half)
-                gns_buf[last, rows], xs_buf[last, rows] = back(last, h * half, half)
-                gn_copy(last, h * half, half, h, flip(last)).start()
-                xs_copy(last, h * half, half, h, flip(last)).start()
-
-    def sweep_sent():
-        def one(c, carry):
-            @pl.when(z < nz - 1)
-            def _():
-                up_copy(c, True).wait_send()
-
-            @pl.when(z > 0)
-            def _():
-                dn_copy(c, True).wait_send()
-
-            return carry
-
-        lax.fori_loop(0, plane, one, 0)
+                back(gns_buf, nd - 1, h * half, half)
+                gn_copy(nd - 1, h * half, half, h, flip(nd - 1)).start()
+
+    def sums_sent(ss, rs, count):
+        moved = p_buf.at[pl.ds(0, count)]
+        remote(moved, moved, ss.at[0], rs.at[0], dev(1 - s, d, z)).wait_send()
 
     def g_copy(o):
-        return remote(g_buf.at[o % nz], gr_buf.at[mine], g_ss.at[o], g_rs.at[mine], dev(0, o // nz, o % nz))
-
-    def g_arrival(o):
-        return remote(g_buf.at[0], gr_buf.at[o], g_ss.at[o], g_rs.at[o], dev(1, d, z))
+        return remote(g_buf.at[o % nz], gr_buf.at[mine], g_ss.at[0], g_rs.at[0], dev(0, o // nz, o % nz))
 
     def g1_copy(j):
-        return remote(g1_buf, gr1_buf.at[j], g1_ss.at[j], g1_rs.at[j], dev(1, flip(j), z))
+        return remote(g1_buf, gr1_buf.at[j], g1_ss.at[0], g1_rs.at[0], dev(1, flip(j), z))
 
     def side_copy(which):
         src, dst = ((infs_buf, infr_buf), (tab_out, tabr_buf))[which]
@@ -739,7 +722,7 @@
     def sc_copy(o):
         to = lax.rem(here + o, column)
         return remote(
-            sc_buf.at[here], sc_buf.at[here], sc_ss.at[o], sc_rs.at[o], dev(to // nz, d, lax.rem(to, nz))
+            sc_buf.at[here], sc_buf.at[here], sc_ss.at[0], sc_rs.at[0], dev(to // nz, d, lax.rem(to, nz))
         )
 
     def score():
@@ -765,7 +748,10 @@
             a_wait(j)
             if j == 1:
                 signal(go_sem.at[0], dev(0, d, z))
-            if j == 2:
+            if j == OGA:
+                og_copy(1).start()
+                og_copy(2).start()
+            if j == OGB:
                 og_copy(3).start()
 
         def on_total(j, q, total):
@@ -794,22 +780,19 @@
             left_buf[zt] = jnp.dot(infr_buf[:, :R], pick_in(zt), preferred_element_type=F32)
         uii_load.wait()
         pl.semaphore_wait(far_sem.at[0], column - 1)
-        for k in range(nz):
-            so_arrival(k).wait_recv()
+        slope_arrival().wait_recv()
         for j in range(1, nd - 1):
             gn_copy(j, 0, tok, 0, d).wait_recv()
-            xs_copy(j, 0, tok, 0, d).wait_recv()
         for k in range(nz):
             if k * 2 % nz == 0:
                 h = k * 2 // nz
                 gn_copy(nd - 1, h * half, half, h, d).wait_recv()
-                xs_copy(nd - 1, h * half, half, h, d).wait_recv()
             rows = pl.ds(k * sub, sub)
-            grad_norm = gnr_buf[0, rows].astype(F32)
-            extra = xr_buf[0, rows].astype(F32)
+            grad_norm = gnr_buf[0, rows, :feat].astype(F32)
+            extra = gnr_buf[0, rows, feat:].astype(F32)
             for j in range(1, nd):
-                grad_norm = grad_norm + gnr_buf[j, rows].astype(F32)
-                extra = extra + xr_buf[j, rows].astype(F32)
+                grad_norm = grad_norm + gnr_buf[j, rows, :feat].astype(F32)
+                extra = extra + gnr_buf[j, rows, feat:].astype(F32)
             dot_buf[0, rows] = extra
             mean_dot = (extra[:, R : R + 1] + extra[:, R + 1 : R + 2]) * (1.0 / width)
             scaled = grad_norm.astype(BF16).astype(F32) * gain_ref[:, pl.ds(z_start, feat)]
@@ -830,8 +813,8 @@
         for j in range(1, nd):
             g1_copy(j).start()
         gr1_buf[0] = own
-        for j in range(1, nd):
-            g1_copy(j).wait_recv()
+        moved = gr1_buf.at[pl.ds(1, nd - 1)]
+        remote(moved, moved, g1_ss.at[0], g1_rs.at[0], dev(0, d, z)).wait_recv()
         for k in range(SEQS):
             row = jnp.zeros((1, piece), F32)
             for group in range(SEQS):
@@ -841,46 +824,93 @@
                 row = row + jnp.where(lax.div(flip(group * per_seq), per_seq) == k, held, 0.0)
             out_ref[k : k + 1, :piece] = row
         score()
-        for j in range(1, nd):
-            og_copy(j).wait_send()
-            g1_copy(j).wait_send()
-        for j in range(1, nd - 1):
-            gn_copy(j, 0, tok, 0, d).wait_send()
-            xs_copy(j, 0, tok, 0, d).wait_send()
-        for h in range(2):
-            gn_copy(nd - 1, h * half, half, h, d).wait_send()
-            xs_copy(nd - 1, h * half, half, h, d).wait_send()
-        for o in range(plane):
-            g_copy(o).wait_send()
+        moved = gns_buf.at[pl.ds(1, nd - 1)]
+        remote(moved, moved, gn_ss.at[0], gn_rs.at[0], dev(0, d, z)).wait_send()
+        moved = og_buf.at[pl.ds(1, nd - 1)]
+        remote(moved, moved, og_ss.at[0], og_rs.at[0], dev(0, d, z)).wait_send()
+        moved = gr1_buf.at[pl.ds(1, nd - 1)]
+        remote(moved, moved, g1_ss.at[0], g1_rs.at[0], dev(0, d, z)).wait_send()
+        remote(gr_buf, gr_buf, g_ss.at[0], g_rs.at[0], dev(0, d, z)).wait_send()
         a_sent()
-        sweep_sent()
+
+        @pl.when(z < nz - 1)
+        def _():
+            sums_sent(up_ss, up_rs, plane)
+
+        @pl.when(z > 0)
+        def _():
+            sums_sent(dn_ss, dn_rs, plane)
+
 
     @pl.when(jnp.logical_not(at_top))
     def _():
-        def chain_up(block, valid):
-            for q in reversed(range(nz)):
-                relay(
-                    block * nz + q, valid, jnp.logical_and(z > 0, q >= z), q > z, up_copy, un_buf, uo_buf
-                )
-
-        def chain_dn(block, valid):
-            for q in range(nz):
-                relay(
-                    block * nz + q, valid, jnp.logical_and(z < nz - 1, q <= z), q < z, dn_copy, dn_buf, do_buf
-                )
+        low = z < nz // 2
+        outer = jnp.logical_or(z == 0, z == nz - 1)
+        inner_z = jnp.where(low, 1, nz - 2)
+        outer_z = jnp.where(low, 0, nz - 1)
+
+        def lift(src, c, to):
+            return remote(src, un_buf.at[c], up_ss.at[0], up_rs.at[c], dev(0, d, to))
+
+        def drop(src, c, to):
+            return remote(src, dn_buf.at[c], dn_ss.at[0], dn_rs.at[c], dev(0, d, to))
+
+        def hand_on(block):
+            for o in range(1, nz):
+                c = block * nz + jnp.where(low, nz - o, o - 1)
+
+                @pl.when(jnp.logical_and(outer, low))
+                def _(c=c):
+                    lift(p_buf.at[c], c, inner_z).start()
+
+                @pl.when(jnp.logical_and(outer, jnp.logical_not(low)))
+                def _(c=c):
+                    drop(p_buf.at[c], c, inner_z).start()
+
+            c = block * nz + outer_z
+
+            @pl.when(jnp.logical_and(jnp.logical_not(outer), low))
+            def _():
+                lift(p_buf.at[c], c, outer_z).start()
+
+            @pl.when(jnp.logical_and(jnp.logical_not(outer), jnp.logical_not(low)))
+            def _():
+                drop(p_buf.at[c], c, outer_z).start()
+
+        def pass_on(block):
+            for o in range(nz // 2):
+                to = jnp.where(low, nz - 1 - o, o)
+                c = block * nz + to
+
+                @pl.when(jnp.logical_and(jnp.logical_not(outer), low))
+                def _(c=c, to=to):
+                    lift(p_buf.at[c], c, to).wait_recv()
+                    uo_buf[c] = (un_buf[c].astype(F32) + p_buf[c].astype(F32)).astype(BF16)
+                    lift(uo_buf.at[c], c, to).start()
+
+                @pl.when(jnp.logical_and(jnp.logical_not(outer), jnp.logical_not(low)))
+                def _(c=c, to=to):
+                    drop(p_buf.at[c], c, to).wait_recv()
+                    uo_buf[c] = (dn_buf[c].astype(F32) + p_buf[c].astype(F32)).astype(BF16)
+                    drop(uo_buf.at[c], c, to).start()
 
         def lower_slope(block):
             c = block * nz + z
-            total = p_buf[c].astype(F32)
-            total = total + jnp.where(z > 0, un_buf[c].astype(F32), 0.0)
-            total = total + jnp.where(z < nz - 1, dn_buf[c].astype(F32), 0.0)
-            so_buf[block] = slope_of(total).astype(BF16)
-            so_copy(block, flip(block)).start()
-
-        far_end = jnp.maximum(z, nz - 1 - z)
+            lift(p_buf.at[c], c, z).wait_recv()
+            drop(p_buf.at[c], c, z).wait_recv()
+            total = p_buf[c].astype(F32) + un_buf[c].astype(F32) + dn_buf[c].astype(F32)
+            so_buf[0, block] = slope_of(total).astype(BF16)
+            if block:
+                so_copy(block).start()
+            else:
+                slope_copy(0).start()
+
+        def forward(block):
+            so_copy(block).wait_recv()
+            slope_copy(block).start()
+
         multiply(0)
-        chain_up(0, z == 0)
-        chain_dn(0, z == nz - 1)
+        hand_on(0)
         infs_buf[:, :R] = in_features()
         infs_buf[:, R:] = jnp.zeros((tok, lanes - R), BF16)
         for which in range(2):
@@ -888,28 +918,22 @@
         pl.semaphore_wait(go_sem.at[0], 1)
         a_start()
         pl.semaphore_wait(far_sem.at[0], column - 1)
-        for hop in range(1, nz):
-            chain_up(0, z == hop)
-            chain_dn(0, nz - 1 - z == hop)
+        pass_on(0)
         lower_slope(0)
         for block in range(1, nd):
             a_wait(block)
             multiply(block)
-            chain_up(block, z == 0)
-            chain_dn(block, z == nz - 1)
-        for step in range(1, nd + nz - 2):
-            block = step + 1 - z
-            chain_up(block, jnp.logical_and(z > 0, jnp.logical_and(block >= 1, block < nd)))
-            block = step + 2 - nz + z
-            chain_dn(block, jnp.logical_and(z < nz - 1, jnp.logical_and(block >= 1, block < nd)))
-            block = step + 1 - far_end
-
-            @pl.when(jnp.logical_and(block >= 1, block < nd))
-            def _(block=block):
-                lower_slope(block)
-
-        for o in range(plane):
-            g_arrival(o).wait_recv()
+            hand_on(block)
+        pass_on(1)
+        for block in range(2, nd):
+            pass_on(block)
+            lower_slope(block - 1)
+            if block > 2:
+                forward(block - 2)
+        lower_slope(nd - 1)
+        for block in range(nd - 2, nd):
+            forward(block)
+        remote(gr_buf, gr_buf, g_ss.at[0], g_rs.at[0], dev(1, d, z)).wait_recv()
         for k in range(SEQS):
             held = gr_buf[k * per_seq * nz]
             for o in range(k * per_seq * nz + 1, (k + 1) * per_seq * nz):
@@ -917,28 +941,27 @@
             out_ref[k : k + 1, :piece] = held
         score()
         a_sent()
-        for j in range(nd):
-            so_copy(j, d).wait_send()
+        moved = so_buf.at[0, pl.ds(1, nd - 1)]
+        remote(moved, moved, so_ss.at[0], so_rs.at[0], dev(1, d, z)).wait_send()
+        slope_arrival().wait_send()
         for which in range(2):
             side_copy(which).wait_send()
-        for j in range(nd):
-            for q in range(nz):
-                @pl.when(q > z)
-                def _(c=j * nz + q):
-                    up_copy(c, True).wait_send()
-
-                @pl.when(q < z)
-                def _(c=j * nz + q):
-                    dn_copy(c, True).wait_send()
-
-    for o in range(1, column):
-        sc_copy(o).wait_recv()
+        @pl.when(low)
+        def _():
+            sums_sent(up_ss, up_rs, nd * (nz - 1))
+
+        @pl.when(jnp.logical_not(low))
+        def _():
+            sums_sent(dn_ss, dn_rs, nd * (nz - 1))
+
+    moved = sc_buf.at[pl.ds(0, column - 1)]
+    others = remote(moved, moved, sc_ss.at[0], sc_rs.at[0], dev(1 - s, d, z))
+    others.wait_recv()
     scores = sc_buf[0]
     for other in range(1, column):
         scores = scores + sc_buf[other]
     out_ref[:, piece : piece + scores.shape[1]] = scores
-    for o in range(1, column):
-        sc_copy(o).wait_send()
+    others.wait_send()
 
 
 def pair_call(nd, nz, tok, width, queries):
@@ -946,12 +969,11 @@
     piece, lanes = R * R // nz, 2 * R
     dma = pltpu.SemaphoreType.DMA
     sems = []
-    for shape in (
-        (nd, 2), (nd,), (plane,), (plane,), (nd, 2), (nd, 2),
-    ):
-        sems += [dma(shape), dma(shape)]
-    sems += [dma((nd,)), dma((nz,)), dma((2,)), dma((2,)), dma((plane,)), dma((plane,))]
-    sems += [dma((nd,)), dma((nd,)), dma((column,)), dma((column,))]
+    for arrivals in (2 * nd - 2, nd - 1, plane, plane, nd, nd - 1, 1):
+        sems += [dma((1,)), dma((arrivals,))]
+    sems += [dma((2,)), dma((2,))]
+    for _ in range(3):
+        sems += [dma((1,)), dma((1,))]
     vmem = pl.BlockSpec(memory_space=pltpu.VMEM)
     hbm = pl.BlockSpec(memory_space=pl.ANY)
     chunks = pltpu.VMEM((plane, sub, cols), BF16)
@@ -974,10 +996,9 @@
             pltpu.VMEM((tok, feat), BF16),
             blocks,
             pltpu.VMEM((nd, tok, lanes), F32),
-            blocks, blocks,
-            pltpu.VMEM((nd, tok, lanes), BF16),
-            pltpu.VMEM((nd, tok, lanes), BF16),
-            pltpu.VMEM((nd, sub, cols), BF16),
+            pltpu.VMEM((nd, tok, feat + lanes), BF16),
+            pltpu.VMEM((nd, tok, feat + lanes), BF16),
+            pltpu.VMEM((2, nd, sub, cols), BF16),
             pltpu.VMEM((nz, sub, cols), BF16),
             pltpu.VMEM((lanes, cols), BF16),
             pltpu.VMEM((tok, lanes), BF16),
@@ -990,7 +1011,7 @@
             pltpu.VMEM((nd, 1, piece), F32),
             pltpu.VMEM((column, SEQS, queries), F32),
             dma((4,)),
-            pltpu.SemaphoreType.REGULAR((2,)),
+            pltpu.SemaphoreType.REGULAR((1,)),
             pltpu.SemaphoreType.REGULAR((1,)),
             *sems,
         ],
@@ -1072,7 +1093,7 @@
     piece = R * R // nz
     queries = query_grads.shape[1]
     vmem = pl.BlockSpec(memory_space=pltpu.VMEM)
-    paired = sections == 2 and nd == 4 and nz % 2 == 0
+    paired = sections == 2 and nd == 4 and nz == 4
     if paired:
         call = pair_call(nd, nz, tok, width, queries)
     else:

time: 56.3 us -> 51.5 us (0.915)
  Pallas kernels: 55.4 us -> 50.6 us
    pallas_call x1, Pallas kernels: 54.8 us -> 50 us  [body(): call(section_input[0], weights[0], gains, proj_seeds, out_grad, query_gra...]
where the time goes in v2:
time: 51.5 us; the launch traced here: 51.3 us
  Pallas kernels  50.6 us (98%)
  between operations  0.64 us (1%)
    pallas_call x1, Pallas kernels, body(): call(section_input[0], weights[0], gains, proj_seeds, out_grad, query_gra...  50 us

profile of v2, /device:TPU:0, one launch (start us, length us, event | category | flops | bytes accessed | tf_op | source)
XLA Modules:
  0.0 51.3 jit_solution(2656703082376812354)
XLA Ops:
  0.6 50.0 %shard_map.77.both_ref = f32[2,1088]{1,0:T(2,128)S(1)} custom-call(bf16[128,4096]{1,0:T(8,128)(2,1)} %bitcast.5, bf16[1024,1024]{1,0:T(8,128)(2,1)} %bitcast.4, f32[1,4096]{1,0:T(1,128)} %gain_ref.1, s32[1,2]{1,0:T(1,128)} %seed_ref.1, bf16[128,4096]{1,0:T(8,128)(2,1)} %og_ref.1, bf16[64,1024]{1,0:T(8,128)(2,1)} %bitcast.6), custom_call_target="tpu_custom_call" | custom-call | tf_op jit(solution)/shard_map/pallas_call | solution.py:1101
  50.7 0.6 %shard_map.78 = (f32[2,1024]{1,0:T(2,128)}, f32[2,64]{1,0:T(2,128)}) custom-call(f32[2,1088]{1,0:T(2,128)S(1)} %shard_map.77.both_ref), custom_call_target="tpu_custom_call" | custom-call | tf_op jit(solution)/shard_map/pallas_call | solution.py:1104

commit v3 on v2

--- a/solution.py
+++ b/solution.py
@@ -17,9 +17,7 @@
 NT = (((1,), (1,)), ((), ()))
 LAG = 6
 GAP = 3
-LATE = 0
-OGA = 1
-OGB = 2
+LOADS = 4
 
 
 def sign_rows(seed_value, row_start, row_count, scale):
@@ -428,10 +426,10 @@
 
 
 def pair_kernel(
-    nd, nz, lag, gap, late,
-    x_hbm, w_hbm, gain_ref, seed_ref, og_ref, q_ref,
+    nd, nz, lag, gap,
+    x_hbm, w_hbm, gain_hbm, seed_ref, og_ref, q_hbm,
     out_ref,
-    x_ref, w_ref, wide_ref, tab_in, tab_out, norm_buf, rad_buf,
+    x_ref, w_ref, gain_ref, q_ref, wide_ref, tab_in, tab_out, norm_buf, rad_buf,
     a_buf, p_buf, un_buf, uo_buf, dn_buf, do_buf,
     og_buf, uii_buf, gp_buf, dot_buf, gns_buf, gnr_buf,
     so_buf, slope_buf, tabr_buf, infs_buf, infr_buf, low_buf,
@@ -481,8 +479,18 @@
 
     x_load = pltpu.make_async_copy(x_hbm, x_ref, in_sem.at[0])
     w_load = pltpu.make_async_copy(w_hbm, w_ref, in_sem.at[1])
-    x_load.start()
-    w_load.start()
+
+    def load(hbm, ref, sem, parts):
+        rows = hbm.shape[0] // parts
+        for part in range(parts):
+            span = pl.ds(part * rows, rows)
+            pltpu.make_async_copy(hbm.at[span], ref.at[span], sem).start()
+
+    gain_load = pltpu.make_async_copy(gain_hbm, gain_ref, in_sem.at[4])
+    q_load = pltpu.make_async_copy(q_hbm, q_ref, in_sem.at[5])
+    load(x_hbm, x_ref, in_sem.at[0], LOADS)
+    gain_load.start()
+    load(w_hbm, w_ref, in_sem.at[1], LOADS)
     barrier = pltpu.get_barrier_semaphore()
 
     def signal_column(sem):
@@ -497,17 +505,11 @@
     ui_load = pltpu.make_async_copy(og_ref.at[:, pl.ds(d_start, cols)], og_buf.at[0], in_sem.at[2])
     uii_load = pltpu.make_async_copy(og_ref.at[:, pl.ds(z_start, feat)], uii_buf, in_sem.at[3])
 
-    @pl.when(at_top)
-    def _():
-        ui_load.start()
-        uii_load.start()
-
     table_row = jnp.where(at_top, d_start, z_start)
     tab_out[:R] = sign_rows(seed_ref[0, 1], table_row, cols, scale)
     tab_out[R:] = jnp.zeros((lanes - R, cols), BF16)
-    tab_in[...] = sign_rows(seed_ref[0, 0], 0, width, scale)
-
     x_load.wait()
+    gain_load.wait()
     hidden = x_ref[...].astype(F32)
     radius = jnp.sqrt(jnp.mean(hidden * hidden, axis=1, keepdims=True) + eps)
     normed_z = x_ref[:, pl.ds(z_start, feat)].astype(F32) / radius
@@ -556,10 +558,15 @@
     def _():
         a_start()
 
+        ui_load.start()
+        uii_load.start()
+
+    q_load.start()
     signal_column(far_sem.at[0])
     w_load.wait()
 
     def in_features():
+        tab_in[...] = sign_rows(seed_ref[0, 0], 0, width, scale)
         lifted = (x_ref[...].astype(F32) / rad_buf[:, :1] * gain_ref[...]).astype(BF16)
         return lax.dot_general(lifted, tab_in[...], NT, preferred_element_type=F32).astype(BF16)
 
@@ -584,7 +591,7 @@
     def gn_copy(j, row, rows, h, to):
         return remote(
             gns_buf.at[j, pl.ds(row, rows)], gnr_buf.at[j, pl.ds(row, rows)],
-            gn_ss.at[0], gn_rs.at[j - 1 + h], dev(s, to, z),
+            gn_ss.at[0], gn_rs.at[2 * j - 2 + h], dev(s, to, z),
         )
 
     def so_copy(j):
@@ -613,8 +620,8 @@
 
     lag_up = z * lag
     lag_dn = (nz - 1 - z) * lag
-    lag_all = jnp.maximum(lag_up, lag_dn) + late
-    slots = plane + gap + (nz - 1) * lag + late
+    lag_all = jnp.maximum(lag_up, lag_dn)
+    slots = plane + gap + (nz - 1) * lag
 
     def chunk_at(v):
         valid = jnp.logical_and(v >= 0, v < plane + gap)
@@ -690,16 +697,11 @@
         def _():
             back(gnr_buf, 0, 0, tok)
 
-        @pl.when(jnp.logical_and(q == nz - 1, jnp.logical_and(j > 0, j < nd - 1)))
-        def _():
-            back(gns_buf, j, 0, tok)
-            gn_copy(j, 0, tok, 0, flip(j)).start()
-
         for h in range(2):
-            @pl.when(jnp.logical_and(q == (h + 1) * nz // 2 - 1, j == nd - 1))
+            @pl.when(jnp.logical_and(q == (h + 1) * nz // 2 - 1, j > 0))
             def _(h=h):
-                back(gns_buf, nd - 1, h * half, half)
-                gn_copy(nd - 1, h * half, half, h, flip(nd - 1)).start()
+                back(gns_buf, j, h * half, half)
+                gn_copy(j, h * half, half, h, flip(j)).start()
 
     def sums_sent(ss, rs, count):
         moved = p_buf.at[pl.ds(0, count)]
@@ -727,6 +729,7 @@
 
     def score():
         grads = out_ref[:, :piece]
+        q_load.wait()
         queries = q_ref[...]
         high = grads.astype(BF16)
         rest = grads - high.astype(F32)
@@ -748,10 +751,14 @@
             a_wait(j)
             if j == 1:
                 signal(go_sem.at[0], dev(0, d, z))
-            if j == OGA:
+            outer = jnp.logical_or(z == 0, z == nz - 1)
+
+            @pl.when(outer if j == 2 else jnp.logical_and(j == 1, jnp.logical_not(outer)))
+            def _():
                 og_copy(1).start()
                 og_copy(2).start()
-            if j == OGB:
+
+            if j == 3:
                 og_copy(3).start()
 
         def on_total(j, q, total):
@@ -781,12 +788,11 @@
         uii_load.wait()
         pl.semaphore_wait(far_sem.at[0], column - 1)
         slope_arrival().wait_recv()
-        for j in range(1, nd - 1):
-            gn_copy(j, 0, tok, 0, d).wait_recv()
         for k in range(nz):
             if k * 2 % nz == 0:
                 h = k * 2 // nz
-                gn_copy(nd - 1, h * half, half, h, d).wait_recv()
+                for j in range(1, nd):
+                    gn_copy(j, h * half, half, h, d).wait_recv()
             rows = pl.ds(k * sub, sub)
             grad_norm = gnr_buf[0, rows, :feat].astype(F32)
             extra = gnr_buf[0, rows, feat:].astype(F32)
@@ -919,11 +925,12 @@
         a_start()
         pl.semaphore_wait(far_sem.at[0], column - 1)
         pass_on(0)
-        lower_slope(0)
         for block in range(1, nd):
             a_wait(block)
             multiply(block)
             hand_on(block)
+            if block == 1:
+                lower_slope(0)
         pass_on(1)
         for block in range(2, nd):
             pass_on(block)
@@ -969,7 +976,7 @@
     piece, lanes = R * R // nz, 2 * R
     dma = pltpu.SemaphoreType.DMA
     sems = []
-    for arrivals in (2 * nd - 2, nd - 1, plane, plane, nd, nd - 1, 1):
+    for arrivals in (2 * nd - 2, nd - 1, plane, plane, 2 * nd - 2, nd - 1, 1):
         sems += [dma((1,)), dma((arrivals,))]
     sems += [dma((2,)), dma((2,))]
     for _ in range(3):
@@ -979,13 +986,15 @@
     chunks = pltpu.VMEM((plane, sub, cols), BF16)
     blocks = pltpu.VMEM((nd, tok, cols), BF16)
     return pl.pallas_call(
-        functools.partial(pair_kernel, nd, nz, LAG, GAP, LATE),
+        functools.partial(pair_kernel, nd, nz, LAG, GAP),
         out_shape=pltpu.VMEM((SEQS, piece + queries), F32),
-        in_specs=[hbm, hbm, vmem, pl.BlockSpec(memory_space=pltpu.SMEM), hbm, vmem],
+        in_specs=[hbm, hbm, hbm, pl.BlockSpec(memory_space=pltpu.SMEM), hbm, hbm],
         out_specs=vmem,
         scratch_shapes=[
             pltpu.VMEM((tok, width), BF16),
             pltpu.VMEM((feat, cols), BF16),
+            pltpu.VMEM((1, width), F32),
+            pltpu.VMEM((queries, piece), BF16),
             pltpu.VMEM((cols, feat + lanes), BF16),
             pltpu.VMEM((R, width), BF16),
             pltpu.VMEM((lanes, cols), BF16),
@@ -1010,7 +1019,7 @@
             pltpu.VMEM((1, piece), F32),
             pltpu.VMEM((nd, 1, piece), F32),
             pltpu.VMEM((column, SEQS, queries), F32),
-            dma((4,)),
+            dma((6,)),
             pltpu.SemaphoreType.REGULAR((1,)),
             pltpu.SemaphoreType.REGULAR((1,)),
             *sems,

time: 51.5 us -> 50.6 us (0.983)
  Pallas kernels: 50.6 us -> 49.8 us
    pallas_call x1, Pallas kernels: 50 us -> 49.2 us  [body(): call(section_input[0], weights[0], gains, proj_seeds, out_grad, query_gra...]
where the time goes in v3:
time: 50.6 us; the launch traced here: 50.5 us
  Pallas kernels  49.8 us (98%)
  between operations  0.64 us (1%)
    pallas_call x1, Pallas kernels, body(): call(section_input[0], weights[0], gains, proj_seeds, out_grad, query_gra...  49.2 us

profile of v3, /device:TPU:0, one launch (start us, length us, event | category | flops | bytes accessed | tf_op | source)
XLA Modules:
  0.0 50.5 jit_solution(16117747056773006820)
XLA Ops:
  0.6 49.2 %shard_map.77.both_ref = f32[2,1088]{1,0:T(2,128)S(1)} custom-call(bf16[128,4096]{1,0:T(8,128)(2,1)} %bitcast.5, bf16[1024,1024]{1,0:T(8,128)(2,1)} %bitcast.4, f32[1,4096]{1,0:T(1,128)} %gain_hbm.1, s32[1,2]{1,0:T(1,128)} %seed_ref.1, bf16[128,4096]{1,0:T(8,128)(2,1)} %og_ref.1, bf16[64,1024]{1,0:T(8,128)(2,1)} %bitcast.6), custom_call_target="tpu_custom_call" | custom-call | tf_op jit(solution)/shard_map/pallas_call | solution.py:1110
  49.9 0.6 %shard_map.78 = (f32[2,1024]{1,0:T(2,128)}, f32[2,64]{1,0:T(2,128)}) custom-call(f32[2,1088]{1,0:T(2,128)S(1)} %shard_map.77.both_ref), custom_call_target="tpu_custom_call" | custom-call | tf_op jit(solution)/shard_map/pallas_call | solution.py:1113

commit v4 on v3

--- a/solution.py
+++ b/solution.py
@@ -433,7 +433,7 @@
     a_buf, p_buf, un_buf, uo_buf, dn_buf, do_buf,
     og_buf, uii_buf, gp_buf, dot_buf, gns_buf, gnr_buf,
     so_buf, slope_buf, tabr_buf, infs_buf, infr_buf, low_buf,
-    left_buf, g_buf, gr_buf, g1_buf, gr1_buf, sc_buf,
+    left_buf, g_buf, gr_buf, g1_buf, gr1_buf, sc_buf, stack_buf,
     in_sem, go_sem, far_sem,
     a_ss, a_rs, og_ss, og_rs, up_ss, up_rs, dn_ss, dn_rs, gn_ss, gn_rs,
     so_ss, so_rs, sl_ss, sl_rs, side_ss, side_rs, g_ss, g_rs, g1_ss, g1_rs, sc_ss, sc_rs,
@@ -731,13 +731,13 @@
         grads = out_ref[:, :piece]
         q_load.wait()
         queries = q_ref[...]
-        high = grads.astype(BF16)
-        rest = grads - high.astype(F32)
-        middle = rest.astype(BF16)
-        low = (rest - middle.astype(F32)).astype(BF16)
-        part = lax.dot_general(high, queries, NT, preferred_element_type=F32)
-        part = part + lax.dot_general(middle, queries, NT, preferred_element_type=F32)
-        part = part + lax.dot_general(low, queries, NT, preferred_element_type=F32)
+        high = grads.astype(BF16).astype(F32)
+        middle = (grads - high).astype(BF16).astype(F32)
+        stack_buf[:SEQS] = high
+        stack_buf[SEQS : 2 * SEQS] = middle
+        stack_buf[2 * SEQS : 3 * SEQS] = grads - high - middle
+        parts = lax.dot_general(stack_buf[...].astype(BF16), queries, NT, preferred_element_type=F32)
+        part = parts[:SEQS] + parts[SEQS : 2 * SEQS] + parts[2 * SEQS : 3 * SEQS]
         sc_buf[here] = part
         for o in range(1, column):
             sc_copy(o).start()
@@ -1019,6 +1019,7 @@
             pltpu.VMEM((1, piece), F32),
             pltpu.VMEM((nd, 1, piece), F32),
             pltpu.VMEM((column, SEQS, queries), F32),
+            pltpu.VMEM((3 * SEQS, piece), F32),
             dma((6,)),
             pltpu.SemaphoreType.REGULAR((1,)),
             pltpu.SemaphoreType.REGULAR((1,)),

time: 50.6 us -> 51.1 us (level)
  no operation moved by 1% of the time
where the time goes in v4:
time: 51.1 us; the launch traced here: 50.9 us
  Pallas kernels  50.3 us (98%)
  between operations  0.64 us (1%)
    pallas_call x1, Pallas kernels, body(): call(section_input[0], weights[0], gains, proj_seeds, out_grad, query_gra...  49.7 us

profile of v4, /device:TPU:0, one launch (start us, length us, event | category | flops | bytes accessed | tf_op | source)
XLA Modules:
  0.0 50.9 jit_solution(3316334467814420519)
XLA Ops:
  0.6 49.7 %shard_map.77.both_ref = f32[2,1088]{1,0:T(2,128)S(1)} custom-call(bf16[128,4096]{1,0:T(8,128)(2,1)} %bitcast.5, bf16[1024,1024]{1,0:T(8,128)(2,1)} %bitcast.4, f32[1,4096]{1,0:T(1,128)} %gain_hbm.1, s32[1,2]{1,0:T(1,128)} %seed_ref.1, bf16[128,4096]{1,0:T(8,128)(2,1)} %og_ref.1, bf16[64,1024]{1,0:T(8,128)(2,1)} %bitcast.6), custom_call_target="tpu_custom_call" | custom-call | tf_op jit(solution)/shard_map/pallas_call | solution.py:1111
  50.3 0.6 %shard_map.78 = (f32[2,1024]{1,0:T(2,128)}, f32[2,64]{1,0:T(2,128)}) custom-call(f32[2,1088]{1,0:T(2,128)S(1)} %shard_map.77.both_ref), custom_call_target="tpu_custom_call" | custom-call | tf_op jit(solution)/shard_map/pallas_call | solution.py:1114
